TPU v7x, 256 devices: a whole 4x4x8 slice. The times are simulated.
256 devices in a mesh: dp: 32 (over y, z_hi, core), factor: 8 (over z_lo, x).
Axes of the slice: x: 4, y: 4, z: 8 (z_hi: 4, z_lo: 2; z = z_hi * 2 + z_lo), core: 2. Of those that a mesh axis runs over, the one named last changes fastest.
Arguments:
- grad_out: bfloat16 [32, 128, 14336], P('dp', None, 'factor'), may hold values from -6 to 6
- act_in: bfloat16 [32, 128, 4096], P('dp', None, 'factor'), may hold values from -6 to 6
- basis_out: bfloat16 [14336, 14336], P('factor', 'dp'), may hold values from -0.046875 to 0.046875
- basis_in: bfloat16 [4096, 4096], P('factor', 'dp'), may hold values from -0.09375 to 0.09375
- eigen_vals: bfloat16 [14336, 4096], P('dp'), may hold values from 0.25 to 4
- query_out: bfloat16 [16, 8, 14336], P(None, None, 'factor'), may hold values from -0.01171875 to 0.01171875
- query_in: bfloat16 [16, 8, 4096], P(None, None, 'factor'), may hold values from -0.01171875 to 0.01171875
Outputs:
- scores: float32 [32, 16], P('factor')
All inputs are finite; a program needn't handle non-finite values.
Results may differ from a plain program's by a relative error of at most 0.023.
Values may be sent and summed in bfloat16 or wider, within the bound.
No kernel may reach another device: no remote copies, remote signals or barrier semaphores. Data moves between devices by JAX's collectives and lax.ppermute only.
A program may use at most 128 MiB of HBM per device.

v0:
```python
import jax
import jax.numpy as jnp
from jax import lax
from jax.sharding import PartitionSpec as P


def shards(grad_out, act_in, basis_out, basis_in, eigen_vals, query_out, query_in):
    shard_part = lax.all_gather(grad_out, "dp", axis=0, tiled=True)
    flattened = shard_part.reshape(-1, shard_part.shape[2])
    product = jnp.dot(flattened, basis_out, preferred_element_type=jnp.float32)
    partial_value = product.reshape(shard_part.shape[0], shard_part.shape[1], -1)
    grad_sum = lax.psum_scatter(
        partial_value.astype(jnp.bfloat16), "factor", scatter_dimension=0, tiled=True
    )
    shard_part = lax.all_gather(act_in, "dp", axis=0, tiled=True)
    flattened = shard_part.reshape(-1, shard_part.shape[2])
    product = jnp.dot(flattened, basis_in, preferred_element_type=jnp.float32)
    act_part = product.reshape(shard_part.shape[0], shard_part.shape[1], -1)
    act_sum = lax.psum_scatter(
        act_part.astype(jnp.bfloat16), "factor", scatter_dimension=0, tiled=True
    )
    act_rot = lax.all_gather(act_sum, "dp", axis=2, tiled=True)
    query_part = jnp.einsum("qrk,ki->qri", query_out, basis_out, preferred_element_type=jnp.float32)
    value_part = jnp.einsum("qrk,kj->qrj", query_in, basis_in, preferred_element_type=jnp.float32)
    query_rot, value_sum = (
        lax.psum(query_part.astype(jnp.bfloat16), "factor").astype(jnp.float32),
        lax.psum(value_part.astype(jnp.bfloat16), "factor").astype(jnp.float32),
    )
    value_rot = lax.all_gather(value_sum.astype(jnp.bfloat16), "dp", axis=2, tiled=True)
    query_count = value_rot.shape[0]
    rank_count = value_rot.shape[1]
    value_mat = value_rot.reshape(query_count * rank_count, value_rot.shape[2])
    eigen_float = eigen_vals.astype(jnp.float32)

    def per_sequence(operands):
        contracted = lax.dot_general(
            operands[0], operands[1], (((0,), (0,)), ((), ())), preferred_element_type=jnp.float32
        )
        scaled = (contracted / eigen_float).astype(jnp.bfloat16)
        weighted = lax.dot_general(
            scaled, value_mat, (((1,), (1,)), ((), ())), preferred_element_type=jnp.float32
        )
        weighted = weighted.reshape(weighted.shape[0], query_count, rank_count)
        return jnp.einsum("iqr,qri->q", weighted, query_rot)

    partial_scores = lax.map(per_sequence, (grad_sum, act_rot))
    return lax.psum(partial_scores, "dp")


def solution(mesh):
    in_specs = (
        P("dp", None, "factor"),
        P("dp", None, "factor"),
        P("factor", "dp"),
        P("factor", "dp"),
        P("dp", None),
        P(None, None, "factor"),
        P(None, None, "factor"),
    )
    out_specs = P("factor", None)
    return jax.shard_map(shards, mesh=mesh, in_specs=in_specs, out_specs=out_specs, check_vma=False)
```

profile of v0, /device:TPU:2, one launch (start us, length us, event | category | flops | bytes accessed | tf_op | source)
XLA Modules:
  0.0 580.7 jit_solution(15563203050592164116)
XLA Ops:
  6.5 0.0 copy-start
  6.5 0.0 copy-start.2
  6.5 0.0 all-gather.7.cloned.1.call-start
  6.5 0.7 all-gather.7.cloned.1.call-update
  7.3 0.0 copy-start.1
  7.3 0.0 copy-start.3
  7.3 0.0 reduce-scatter.5.cloned.1.call-start
  7.3 65.9 %all-gather.7.cloned.1.call-done = bf16[32,128,512]{2,1,0:T(8,128)(2,1)} async-done(((bf16[1,128,512]{2,1,0:T(8,128)(2,1)}), bf16[32,128,512]{2,1,0:T(8,128)(2,1)}) %all-gather.7.cloned.1.call-update) | async-done | bytes 4194320 | tf_op jit(solution)/shard_map/all_gather | solution.py:15
  73.2 4.4 convolution_convert_fusion.1
  77.6 0.0 reduce-scatter.5.cloned.1.call-update
  77.7 0.0 all-gather.5.cloned.1.call-start
  77.7 0.7 all-gather.5.cloned.1.call-update
  78.4 0.0 all-reduce.2.cloned.1.call-start
  78.5 0.0 copy-done
  78.5 0.0 copy-done.2
  78.5 1.3 fusion.17
  79.7 0.0 all-reduce.2.cloned.1.call-update
  79.8 0.0 all-gather.11.cloned.1.call-start
  79.8 0.0 copy-done.1
  79.8 0.0 copy-done.3
  79.8 0.2 convolution_convert_fusion.2
  80.0 30.1 %psum.21 = bf16[16,8,128]{2,1,0:T(8,128)(2,1)} all-reduce(bf16[16,8,128]{2,1,0:T(8,128)(2,1)S(1)} %convolution_convert_fusion.2), channel_id=1, replica_groups=mesh['dp'=32,'factor'=8] {'factor'}, use_global_device_ids=true, to_apply=%region_2.0 | all-reduce | flops 16384 | bytes 65536 | tf_op jit(solution)/shard_map/psum | solution.py:27
  110.1 0.0 all-gather.11.cloned.1.call-update
  110.1 0.0 all-gather.9.cloned.1.call-start
  110.2 5.2 reduce-scatter.5.cloned.1.call-done
  115.4 0.0 all-gather.9.cloned.1.call-update
  115.4 0.0 reduce-scatter.3.cloned.1.call-start
  115.4 101.9 %all-gather.5.cloned.1.call-done = bf16[32,128,1792]{2,1,0:T(8,128)(2,1)} async-done(((bf16[1,128,1792]{2,1,0:T(8,128)(2,1)}), bf16[32,128,1792]{2,1,0:T(8,128)(2,1)}) %all-gather.5.cloned.1.call-update) | async-done | bytes 14680080 | tf_op jit(solution)/shard_map/all_gather | solution.py:8
  217.4 11.6 %convolution_convert_fusion = bf16[32,128,448]{1,2,0:T(8,128)(2,1)} fusion(bf16[32,128,1792]{2,1,0:T(8,128)(2,1)} %all-gather.5.cloned.1.call-done, bf16[1792,448]{0,1:T(8,128)(2,1)S(1)} %copy-done), kind=kOutput, calls=%fused_computation.10 | convolution fusion | flops 6578503680 | bytes 19955712 | tf_op jit(solution)/shard_map/dot_general | solution.py:10
  229.0 0.0 reduce-scatter.3.cloned.1.call-update
  229.0 5.9 %convert_element_type.25 = f32[448,4096]{1,0:T(8,128)} convert(bf16[448,4096]{1,0:T(8,128)(2,1)} %param.13) | non-fusion elementwise | flops 1835008 | bytes 11010048 | tf_op jit(solution)/shard_map/convert_element_type | solution.py:33
  234.9 71.2 %all-reduce.2.cloned.1.call-done = bf16[16,8,448]{2,1,0:T(8,128)(2,1)} async-done(((bf16[16,8,448]{2,1,0:T(8,128)(2,1)}), bf16[16,8,448]{2,1,0:T(8,128)(2,1)}) %all-reduce.2.cloned.1.call-update) | async-done | bytes 114704 | tf_op jit(solution)/shard_map/psum | solution.py:26
  306.1 0.9 convert_element_type.28
  307.0 55.1 %all-gather.11.cloned.1.call-done = bf16[16,8,4096]{2,1,0:T(8,128)(2,1)} async-done(((bf16[16,8,128]{2,1,0:T(8,128)(2,1)}), bf16[16,8,4096]{2,1,0:T(8,128)(2,1)}) %all-gather.11.cloned.1.call-update) | async-done | bytes 1048592 | tf_op jit(solution)/shard_map/all_gather | solution.py:29
  362.1 63.3 %all-gather.9.cloned.1.call-done = bf16[4,128,4096]{2,1,0:T(8,128)(2,1)} async-done(((bf16[4,128,128]{2,1,0:T(8,128)(2,1)}), bf16[4,128,4096]{2,1,0:T(8,128)(2,1)}) %all-gather.9.cloned.1.call-update) | async-done | bytes 4194320 | tf_op jit(solution)/shard_map/all_gather | solution.py:22
  425.5 50.1 %reduce-scatter.3.cloned.1.call-done = bf16[4,128,448]{1,2,0:T(8,128)(2,1)} async-done(((bf16[32,128,448]{1,2,0:T(8,128)(2,1)}), bf16[4,128,448]{1,2,0:T(8,128)(2,1)}) %reduce-scatter.3.cloned.1.call-update) | async-done | bytes 458768 | tf_op jit(solution)/shard_map/reduce_scatter | solution.py:12
  475.6 24.1 %while.10 = (s32[]{:T(128)}, f32[4,16]{1,0:T(4,128)S(1)}, bf16[4,128,448]{1,2,0:T(8,128)(2,1)}, bf16[4,128,4096]{2,1,0:T(8,128)(2,1)}, f32[448,4096]{1,0:T(8,128...) while((s32[]{:T(128)}, f32[4,16]{1,0:T(4,128)S(1)}, ...), condition=%wide.region_5.6_spmd, body=%wide.region_4.5_spmd.sunk | while | flops 943308800 | bytes 9782569 | solution.py:46
  475.6 6.0 %fusion.34 = f32[16]{0:T(128)S(1)} fusion(bf16[128,4096]{1,0:T(8,128)(2,1)} %get-tuple-element.144, f32[448,4096]{1,0:T(8,128)} %get-tuple-element.143, bf16[4,128,4096]{2,1,0:T(8,128)(2,1)} %get-tuple-element.142, s32[]{:T(128)S(6)} %copy.25, f32[16,8,448]{2,1,0:T(8,128)S(1)} %get-tuple-element.145, bf16[4,128,448]{1,2,0:T(8,128)(2,1)} %get-tuple-element.141), kind=kOutput, calls=%fused_computation.4.clone.1 | convolution fusion | flops 943308800 | bytes 9782336 | tf_op jit(solution)/shard_map/while/body/eval_jaxpr/dot_general | solution.py:40
  481.6 6.0 %fusion.34 = f32[16]{0:T(128)S(1)} fusion(bf16[128,4096]{1,0:T(8,128)(2,1)} %get-tuple-element.144, f32[448,4096]{1,0:T(8,128)} %get-tuple-element.143, bf16[4,128,4096]{2,1,0:T(8,128)(2,1)} %get-tuple-element.142, s32[]{:T(128)S(6)} %copy.25, f32[16,8,448]{2,1,0:T(8,128)S(1)} %get-tuple-element.145, bf16[4,128,448]{1,2,0:T(8,128)(2,1)} %get-tuple-element.141), kind=kOutput, calls=%fused_computation.4.clone.1 | convolution fusion | flops 943308800 | bytes 9782336 | tf_op jit(solution)/shard_map/while/body/eval_jaxpr/dot_general | solution.py:40
  487.6 6.0 %fusion.34 = f32[16]{0:T(128)S(1)} fusion(bf16[128,4096]{1,0:T(8,128)(2,1)} %get-tuple-element.144, f32[448,4096]{1,0:T(8,128)} %get-tuple-element.143, bf16[4,128,4096]{2,1,0:T(8,128)(2,1)} %get-tuple-element.142, s32[]{:T(128)S(6)} %copy.25, f32[16,8,448]{2,1,0:T(8,128)S(1)} %get-tuple-element.145, bf16[4,128,448]{1,2,0:T(8,128)(2,1)} %get-tuple-element.141), kind=kOutput, calls=%fused_computation.4.clone.1 | convolution fusion | flops 943308800 | bytes 9782336 | tf_op jit(solution)/shard_map/while/body/eval_jaxpr/dot_general | solution.py:40
  493.6 6.0 %fusion.34 = f32[16]{0:T(128)S(1)} fusion(bf16[128,4096]{1,0:T(8,128)(2,1)} %get-tuple-element.144, f32[448,4096]{1,0:T(8,128)} %get-tuple-element.143, bf16[4,128,4096]{2,1,0:T(8,128)(2,1)} %get-tuple-element.142, s32[]{:T(128)S(6)} %copy.25, f32[16,8,448]{2,1,0:T(8,128)S(1)} %get-tuple-element.145, bf16[4,128,448]{1,2,0:T(8,128)(2,1)} %get-tuple-element.141), kind=kOutput, calls=%fused_computation.4.clone.1 | convolution fusion | flops 943308800 | bytes 9782336 | tf_op jit(solution)/shard_map/while/body/eval_jaxpr/dot_general | solution.py:40
  499.7 74.2 %psum.23 = f32[4,16]{1,0:T(4,128)} all-reduce(f32[4,16]{1,0:T(4,128)S(1)} %get-tuple-element.42), channel_id=1, replica_groups=mesh['dp'=32,'factor'=8] {'dp'}, use_global_device_ids=true, to_apply=%region_6.7 | all-reduce | flops 64 | bytes 512 | tf_op jit(solution)/shard_map/psum | solution.py:47
  (5 shorter events, 0.1 us)
Async XLA Ops:
  6.5 71.9 %copy-start = (bf16[1792,448]{0,1:T(8,128)(2,1)S(1)}, bf16[1792,448]{0,1:T(8,128)(2,1)}, u32[]{:S(2)}) copy-start(bf16[1792,448]{0,1:T(8,128)(2,1)} %param.11) | copy-start | bytes 4816900
  6.5 71.9 %copy-start.2 = (bf16[16,8,1792]{2,1,0:T(8,128)(2,1)S(1)}, bf16[16,8,1792]{2,1,0:T(8,128)(2,1)}, u32[]{:S(2)}) copy-start(bf16[16,8,1792]{2,1,0:T(8,128)(2,1)} %param.14) | copy-start | bytes 1376260
  6.5 66.7 %all-gather.7.cloned.1.call-start = ((), (), s32[]{:S(2)}) async-start(), calls=%async_computation.4 | async-start | bytes 4325376 | tf_op jit(solution)/shard_map/all_gather | solution.py:15
  7.3 72.6 %copy-start.1 = (bf16[512,128]{1,0:T(8,128)(2,1)S(1)}, bf16[512,128]{1,0:T(8,128)(2,1)}, u32[]{:S(2)}) copy-start(bf16[512,128]{1,0:T(8,128)(2,1)} %param.12) | copy-start | bytes 393220
  7.3 72.6 %copy-start.3 = (bf16[16,8,512]{2,1,0:T(8,128)(2,1)S(1)}, bf16[16,8,512]{2,1,0:T(8,128)(2,1)}, u32[]{:S(2)}) copy-start(bf16[16,8,512]{2,1,0:T(8,128)(2,1)} %param.15) | copy-start | bytes 393220
  7.3 108.1 %reduce-scatter.5.cloned.1.call-start = ((), (), s32[]{:S(2)}) async-start(), calls=%async_computation.5 | async-start | bytes 1179648 | tf_op jit(solution)/shard_map/reduce_scatter | solution.py:19
  77.7 139.7 %all-gather.5.cloned.1.call-start = ((), (), s32[]{:S(2)}) async-start(), calls=%async_computation.2 | async-start | bytes 15138816 | tf_op jit(solution)/shard_map/all_gather | solution.py:8
  78.4 227.7 %all-reduce.2.cloned.1.call-start = ((), (), s32[]{:S(2)}) async-start(), calls=%async_computation.8 | async-start | bytes 262144 | tf_op jit(solution)/shard_map/psum | solution.py:26
  79.8 282.4 %all-gather.11.cloned.1.call-start = ((), (), s32[]{:S(2)}) async-start(), calls=%async_computation.7 | async-start | bytes 1081344 | tf_op jit(solution)/shard_map/all_gather | solution.py:29
  110.1 315.4 %all-gather.9.cloned.1.call-start = ((), (), s32[]{:S(2)}) async-start(), calls=%async_computation.6 | async-start | bytes 4325376 | tf_op jit(solution)/shard_map/all_gather | solution.py:22
  115.4 360.2 %reduce-scatter.3.cloned.1.call-start = ((), (), s32[]{:S(2)}) async-start(), calls=%async_computation.3 | async-start | bytes 4128768 | tf_op jit(solution)/shard_map/reduce_scatter | solution.py:12
Sparse Core Ops, SparseCore 0:
  9.9 63.2 all-gather.6
  77.8 37.5 reduce-scatter.4
  117.9 99.4 all-gather.4
  219.8 86.1 all-reduce.1
  308.4 53.7 all-gather.10
  364.5 60.9 all-gather.8
  428.0 47.4 reduce-scatter.2
where the time goes:
time: 581 us
  waiting for transfers between devices  414 us (71%)
  blocking collectives  104 us (18%)
  matrix products  41.4 us (7%)
  between operations  13.6 us (2%)
  other arithmetic  6.81 us (1%)
    all_gather x1, waiting for transfers between devices, shards(): shard_part = lax.all_gather(grad_out, 'dp', axis=0, tiled=True)  102 us
    psum x1, blocking collectives, shards(): return lax.psum(partial_scores, 'dp')  74.2 us
    psum x1, waiting for transfers between devices, shards(): lax.psum(query_part.astype(jnp.bfloat16), 'factor').astype(jnp.float32)  71.2 us
    all_gather x1, waiting for transfers between devices, shards(): shard_part = lax.all_gather(act_in, 'dp', axis=0, tiled=True)  65.9 us
    all_gather x1, waiting for transfers between devices, shards(): act_rot = lax.all_gather(act_sum, 'dp', axis=2, tiled=True)  63.3 us
    all_gather x1, waiting for transfers between devices, shards(): lax.all_gather(value_sum.astype(jnp.bfloat16), 'dp', axis=2, tiled=True)  55.1 us
    reduce_scatter x1, waiting for transfers between devices, shards(): lax.psum_scatter(partial_value.astype(jnp.bfloat16), 'factor', scatter_di...  50.1 us
    psum x1, blocking collectives, shards(): lax.psum(value_part.astype(jnp.bfloat16), 'factor').astype(jnp.float32)  30.1 us
  transfers between devices with their start and end apart: 7, of which 7 were waited for; matrix products, arithmetic and copies ran while one was open for 3% of the time, Pallas kernels for 0%

commit v1 on v0

--- a/solution.py
+++ b/solution.py
@@ -12,7 +12,9 @@
     grad_sum = lax.psum_scatter(
         partial_value.astype(jnp.bfloat16), "factor", scatter_dimension=0, tiled=True
     )
-    shard_part = lax.all_gather(act_in, "dp", axis=0, tiled=True)
+    shard_part = jnp.concatenate(
+        lax.all_to_all(jnp.stack([act_in] * lax.axis_size("dp")), "dp", 0, 0), axis=0
+    )
     flattened = shard_part.reshape(-1, shard_part.shape[2])
     product = jnp.dot(flattened, basis_in, preferred_element_type=jnp.float32)
     act_part = product.reshape(shard_part.shape[0], shard_part.shape[1], -1)

time: 581 us -> 466 us (0.80); the launches traced: 581 us -> 458 us
  waiting for transfers between devices: 414 us -> 182 us
  blocking collectives: 104 us -> 212 us
    all_to_all x0 -> x1, blocking collectives: none -> 106 us  [shards(): lax.all_to_all(jnp.stack([act_in] * lax.axis_size('dp')), 'dp', 0, 0)]
    all_gather x1 -> x0, waiting for transfers between devices: 65.9 us -> none  [shards(): shard_part = lax.all_gather(act_in, 'dp', axis=0, tiled=True)]
    all_gather x1, waiting for transfers between devices: 55.1 us -> 0.03 us  [shards(): lax.all_gather(value_sum.astype(jnp.bfloat16), 'dp', axis=2, tiled=True)]
    reduce_scatter x1, waiting for transfers between devices: 50.1 us -> 1.48 us  [shards(): lax.psum_scatter(partial_value.astype(jnp.bfloat16), 'factor', scatter_di...]
    all_gather x1, waiting for transfers between devices: 102 us -> 53.7 us  [shards(): shard_part = lax.all_gather(grad_out, 'dp', axis=0, tiled=True)]
    psum x1, waiting for transfers between devices: 71.2 us -> 49.5 us  [shards(): lax.psum(query_part.astype(jnp.bfloat16), 'factor').astype(jnp.float32)]
    reduce_scatter x1, waiting for transfers between devices: 5.17 us -> 12.1 us  [shards(): lax.psum_scatter(act_part.astype(jnp.bfloat16), 'factor', scatter_dimensi...]
  transfers between devices with their start and end apart: 7 -> 6, of which waited for: 7 -> 5; matrix products, arithmetic and copies ran while one was open for 3% -> 4% of each run, Pallas kernels for 0% -> 0%
where the time goes in v1:
time: 466 us; the launch traced here: 458 us
  blocking collectives  212 us (45%)
  waiting for transfers between devices  182 us (39%)
  matrix products  39.2 us (8%)
  between operations  14.9 us (3%)
  other arithmetic  6.81 us (1%)
    all_to_all x1, blocking collectives, shards(): lax.all_to_all(jnp.stack([act_in] * lax.axis_size('dp')), 'dp', 0, 0)  106 us
    psum x1, blocking collectives, shards(): return lax.psum(partial_scores, 'dp')  72.7 us
    all_gather x1, waiting for transfers between devices, shards(): act_rot = lax.all_gather(act_sum, 'dp', axis=2, tiled=True)  64.8 us
    all_gather x1, waiting for transfers between devices, shards(): shard_part = lax.all_gather(grad_out, 'dp', axis=0, tiled=True)  53.7 us
    psum x1, waiting for transfers between devices, shards(): lax.psum(query_part.astype(jnp.bfloat16), 'factor').astype(jnp.float32)  49.5 us
    psum x1, blocking collectives, shards(): lax.psum(value_part.astype(jnp.bfloat16), 'factor').astype(jnp.float32)  34.2 us
    dot_general x4, matrix products, per_sequence(): lax.dot_general(scaled, value_mat, (((1,), (1,)), ((), ())), preferred_el...  23.9 us
    reduce_scatter x1, waiting for transfers between devices, shards(): lax.psum_scatter(act_part.astype(jnp.bfloat16), 'factor', scatter_dimensi...  12.1 us
  transfers between devices with their start and end apart: 6, of which 5 were waited for; matrix products, arithmetic and copies ran while one was open for 4% of the time, Pallas kernels for 0%

profile of v1, /device:TPU:2, one launch (start us, length us, event | category | flops | bytes accessed | tf_op | source)
XLA Modules:
  0.0 457.5 jit_solution(14056458425171123841)
XLA Ops:
  7.4 0.0 copy-start
  7.4 0.0 reduce-scatter.5.cloned.1.call-start
  7.4 1.5 stack.2
  8.9 0.0 copy-start.1
  8.9 105.5 %all_to_all.5 = bf16[32,1,128,512]{3,2,1,0:T(8,128)(2,1)S(1)} all-to-all(bf16[32,1,128,512]{3,2,1,0:T(8,128)(2,1)S(1)} %stack.2), channel_id=1, replica_groups=mesh['dp'=32,'factor'=8] {'dp'}, dimensions={0} | all-to-all | bytes 8388608 | tf_op jit(solution)/shard_map/all_to_all | solution.py:16
  114.4 0.0 copy-done.1
  114.4 0.0 copy-start.2
  114.4 0.0 copy-start.3
  114.4 2.3 fusion.19
  116.7 0.0 reduce-scatter.5.cloned.1.call-update
  116.7 0.0 all-gather.4.cloned.1.call-start
  116.8 0.5 all-gather.4.cloned.1.call-update
  117.3 0.0 all-reduce.2.cloned.1.call-start
  117.3 0.0 copy-done
  117.4 0.0 copy-done.2
  117.4 1.3 fusion.22
  118.6 0.0 all-reduce.2.cloned.1.call-update
  118.6 0.0 all-gather.8.cloned.1.call-start
  118.7 0.0 copy-done.3
  118.7 0.2 convolution_convert_fusion.1
  118.9 34.2 %psum.21 = bf16[16,8,128]{2,1,0:T(8,128)(2,1)} all-reduce(bf16[16,8,128]{2,1,0:T(8,128)(2,1)S(1)} %convolution_convert_fusion.1), channel_id=1, replica_groups=mesh['dp'=32,'factor'=8] {'factor'}, use_global_device_ids=true, to_apply=%region_2.0 | all-reduce | flops 16384 | bytes 65536 | tf_op jit(solution)/shard_map/psum | solution.py:29
  153.1 0.0 all-gather.8.cloned.1.call-update
  153.1 0.0 all-gather.6.cloned.1.call-start
  153.2 12.1 %reduce-scatter.5.cloned.1.call-done = bf16[4,128,128]{2,1,0:T(8,128)(2,1)} async-done(((bf16[32,128,128]{2,1,0:T(8,128)(2,1)}), bf16[4,128,128]{2,1,0:T(8,128)(2,1)}) %reduce-scatter.5.cloned.1.call-update) | async-done | bytes 131088 | tf_op jit(solution)/shard_map/reduce_scatter | solution.py:21
  165.3 0.0 all-gather.6.cloned.1.call-update
  165.3 0.0 reduce-scatter.3.cloned.1.call-start
  165.4 53.7 %all-gather.4.cloned.1.call-done = bf16[32,128,1792]{2,1,0:T(8,128)(2,1)} async-done(((bf16[1,128,1792]{2,1,0:T(8,128)(2,1)}), bf16[32,128,1792]{2,1,0:T(8,128)(2,1)}) %all-gather.4.cloned.1.call-update) | async-done | bytes 14680080 | tf_op jit(solution)/shard_map/all_gather | solution.py:8
  219.1 11.6 %convolution_convert_fusion = bf16[32,128,448]{1,2,0:T(8,128)(2,1)} fusion(bf16[32,128,1792]{2,1,0:T(8,128)(2,1)} %all-gather.4.cloned.1.call-done, bf16[1792,448]{0,1:T(8,128)(2,1)S(1)} %copy-done), kind=kOutput, calls=%fused_computation.12 | convolution fusion | flops 6578503680 | bytes 19955712 | tf_op jit(solution)/shard_map/dot_general | solution.py:10
  230.7 0.0 reduce-scatter.3.cloned.1.call-update
  230.7 5.9 %convert_element_type.25 = f32[448,4096]{1,0:T(8,128)} convert(bf16[448,4096]{1,0:T(8,128)(2,1)} %param.13) | non-fusion elementwise | flops 1835008 | bytes 11010048 | tf_op jit(solution)/shard_map/convert_element_type | solution.py:35
  236.6 49.5 %all-reduce.2.cloned.1.call-done = bf16[16,8,448]{2,1,0:T(8,128)(2,1)} async-done(((bf16[16,8,448]{2,1,0:T(8,128)(2,1)}), bf16[16,8,448]{2,1,0:T(8,128)(2,1)}) %all-reduce.2.cloned.1.call-update) | async-done | bytes 114704 | tf_op jit(solution)/shard_map/psum | solution.py:28
  286.2 0.9 convert_element_type.28
  287.1 0.0 all-gather.8.cloned.1.call-done
  287.1 64.8 %all-gather.6.cloned.1.call-done = bf16[4,128,4096]{2,1,0:T(8,128)(2,1)} async-done(((bf16[4,128,128]{2,1,0:T(8,128)(2,1)}), bf16[4,128,4096]{2,1,0:T(8,128)(2,1)}) %all-gather.6.cloned.1.call-update) | async-done | bytes 4194320 | tf_op jit(solution)/shard_map/all_gather | solution.py:24
  351.9 1.5 reduce-scatter.3.cloned.1.call-done
  353.4 24.1 %while.10 = (s32[]{:T(128)}, f32[4,16]{1,0:T(4,128)S(1)}, bf16[4,128,448]{1,2,0:T(8,128)(2,1)}, bf16[4,128,4096]{2,1,0:T(8,128)(2,1)}, f32[448,4096]{1,0:T(8,128...) while((s32[]{:T(128)}, f32[4,16]{1,0:T(4,128)S(1)}, ...), condition=%wide.region_5.6_spmd, body=%wide.region_4.5_spmd.sunk | while | flops 943308800 | bytes 9782569 | solution.py:48
  353.4 6.0 %fusion.38 = f32[16]{0:T(128)S(1)} fusion(bf16[128,4096]{1,0:T(8,128)(2,1)} %get-tuple-element.144, f32[448,4096]{1,0:T(8,128)} %get-tuple-element.143, bf16[4,128,4096]{2,1,0:T(8,128)(2,1)} %get-tuple-element.142, s32[]{:T(128)S(6)} %copy.25, f32[16,8,448]{2,1,0:T(8,128)S(1)} %get-tuple-element.145, bf16[4,128,448]{1,2,0:T(8,128)(2,1)} %get-tuple-element.141), kind=kOutput, calls=%fused_computation.4.clone.1 | convolution fusion | flops 943308800 | bytes 9782336 | tf_op jit(solution)/shard_map/while/body/eval_jaxpr/dot_general | solution.py:42
  359.4 6.0 %fusion.38 = f32[16]{0:T(128)S(1)} fusion(bf16[128,4096]{1,0:T(8,128)(2,1)} %get-tuple-element.144, f32[448,4096]{1,0:T(8,128)} %get-tuple-element.143, bf16[4,128,4096]{2,1,0:T(8,128)(2,1)} %get-tuple-element.142, s32[]{:T(128)S(6)} %copy.25, f32[16,8,448]{2,1,0:T(8,128)S(1)} %get-tuple-element.145, bf16[4,128,448]{1,2,0:T(8,128)(2,1)} %get-tuple-element.141), kind=kOutput, calls=%fused_computation.4.clone.1 | convolution fusion | flops 943308800 | bytes 9782336 | tf_op jit(solution)/shard_map/while/body/eval_jaxpr/dot_general | solution.py:42
  365.4 6.0 %fusion.38 = f32[16]{0:T(128)S(1)} fusion(bf16[128,4096]{1,0:T(8,128)(2,1)} %get-tuple-element.144, f32[448,4096]{1,0:T(8,128)} %get-tuple-element.143, bf16[4,128,4096]{2,1,0:T(8,128)(2,1)} %get-tuple-element.142, s32[]{:T(128)S(6)} %copy.25, f32[16,8,448]{2,1,0:T(8,128)S(1)} %get-tuple-element.145, bf16[4,128,448]{1,2,0:T(8,128)(2,1)} %get-tuple-element.141), kind=kOutput, calls=%fused_computation.4.clone.1 | convolution fusion | flops 943308800 | bytes 9782336 | tf_op jit(solution)/shard_map/while/body/eval_jaxpr/dot_general | solution.py:42
  371.5 6.0 %fusion.38 = f32[16]{0:T(128)S(1)} fusion(bf16[128,4096]{1,0:T(8,128)(2,1)} %get-tuple-element.144, f32[448,4096]{1,0:T(8,128)} %get-tuple-element.143, bf16[4,128,4096]{2,1,0:T(8,128)(2,1)} %get-tuple-element.142, s32[]{:T(128)S(6)} %copy.25, f32[16,8,448]{2,1,0:T(8,128)S(1)} %get-tuple-element.145, bf16[4,128,448]{1,2,0:T(8,128)(2,1)} %get-tuple-element.141), kind=kOutput, calls=%fused_computation.4.clone.1 | convolution fusion | flops 943308800 | bytes 9782336 | tf_op jit(solution)/shard_map/while/body/eval_jaxpr/dot_general | solution.py:42
  377.5 72.7 %psum.23 = f32[4,16]{1,0:T(4,128)} all-reduce(f32[4,16]{1,0:T(4,128)S(1)} %get-tuple-element.42), channel_id=1, replica_groups=mesh['dp'=32,'factor'=8] {'dp'}, use_global_device_ids=true, to_apply=%region_6.7 | all-reduce | flops 64 | bytes 512 | tf_op jit(solution)/shard_map/psum | solution.py:49
  (5 shorter events, 0.1 us)
Async XLA Ops:
  7.4 110.0 %copy-start = (bf16[1792,448]{0,1:T(8,128)(2,1)S(1)}, bf16[1792,448]{0,1:T(8,128)(2,1)}, u32[]{:S(2)}) copy-start(bf16[1792,448]{0,1:T(8,128)(2,1)} %param.11) | copy-start | bytes 4816900
  7.4 157.9 %reduce-scatter.5.cloned.1.call-start = ((), (), s32[]{:S(2)}) async-start(), calls=%async_computation.5 | async-start | bytes 1179648 | tf_op jit(solution)/shard_map/reduce_scatter | solution.py:21
  8.9 105.6 %copy-start.1 = (bf16[512,128]{1,0:T(8,128)(2,1)S(1)}, bf16[512,128]{1,0:T(8,128)(2,1)}, u32[]{:S(2)}) copy-start(bf16[512,128]{1,0:T(8,128)(2,1)} %param.12) | copy-start | bytes 393220
  114.4 2.9 copy-start.2
  114.4 4.3 copy-start.3
  116.7 102.4 %all-gather.4.cloned.1.call-start = ((), (), s32[]{:S(2)}) async-start(), calls=%async_computation.3 | async-start | bytes 15138816 | tf_op jit(solution)/shard_map/all_gather | solution.py:8
  117.3 168.9 %all-reduce.2.cloned.1.call-start = ((), (), s32[]{:S(2)}) async-start(), calls=%async_computation.8 | async-start | bytes 262144 | tf_op jit(solution)/shard_map/psum | solution.py:28
  118.6 168.5 %all-gather.8.cloned.1.call-start = ((), (), s32[]{:S(2)}) async-start(), calls=%async_computation.7 | async-start | bytes 1081344 | tf_op jit(solution)/shard_map/all_gather | solution.py:31
  153.1 198.8 %all-gather.6.cloned.1.call-start = ((), (), s32[]{:S(2)}) async-start(), calls=%async_computation.6 | async-start | bytes 4325376 | tf_op jit(solution)/shard_map/all_gather | solution.py:24
  165.3 188.1 %reduce-scatter.3.cloned.1.call-start = ((), (), s32[]{:S(2)}) async-start(), calls=%async_computation.4 | async-start | bytes 4128768 | tf_op jit(solution)/shard_map/reduce_scatter | solution.py:12
Sparse Core Ops, SparseCore 0:
  116.8 48.4 reduce-scatter.4
  167.9 118.2 all-reduce.1
  288.7 64.6 reduce-scatter.2
Sparse Core Ops, SparseCore 1:
  119.7 99.3 all-gather.3
  221.4 61.3 all-gather.7
  285.1 66.7 all-gather.5
